TPU v7x, 256 devices: a whole 4x4x8 slice. The times are simulated.
256 devices in a mesh: row: 4 (over y_lo, core), col: 2 (over y_hi), env: 32 (over x, z).
Axes of the slice: x: 4, y: 4 (y_hi: 2, y_lo: 2; y = y_hi * 2 + y_lo), z: 8, core: 2. Of those that a mesh axis runs over, the one named last changes fastest.
Arguments:
- corner: bfloat16 [4, 2, 1024, 1024], P('row', 'col'), may hold values from -0.1875 to 0.1875
- top_edge: bfloat16 [4, 2, 1024, 32768], P('row', 'col', 'env'), may hold values from -0.03125 to 0.03125
- half_system: bfloat16 [4, 2, 1024, 32768], P('row', 'col', 'env'), may hold values from -0.03125 to 0.03125
- values: float32 [4, 2, 1024], P('row', 'col'), may hold values from 0.5 to 4
- cotangent: bfloat16 [4, 2, 1024, 1024], P('row', 'col'), may hold values from -32 to 32
- parity: int32 [4, 2, 4, 8], P('row', 'col'), may hold values 0 or 1
Outputs:
- grad_corner: bfloat16 [4, 2, 1024, 1024], P('row', 'col', 'env')
- grad_edge: bfloat16 [4, 2, 1024, 32768], P('row', 'col', 'env')
- grad_half: bfloat16 [4, 2, 1024, 32768], P('row', 'col', 'env')
- grad_values: float32 [4, 2, 1024], P('row', 'col', 'env')
Inputs may be any that keep to these rules, and one draw needn't show every extreme that they name: `parity`: each entry is the Z2 charge of one block of 128 environment indices.
All inputs are finite; a program needn't handle non-finite values.
Results may differ from a plain program's by a relative error of at most 0.0058.
Values may be sent and summed in bfloat16 or wider, within the bound.
A program may use at most 128 MiB of HBM per device.

v0:
```python
import jax
import jax.numpy as jnp
from jax import lax
from jax.sharding import PartitionSpec as P

CHI = 1024
HALF = 32
BLK = 128


def passed_along(x, axis, by):
    size = lax.axis_size(axis)
    return lax.ppermute(x, axis, [(i, (i + by) % size) for i in range(size)])


def side_column(tensor, direction):
    return passed_along(tensor, "col", direction)


def side_row(tensor, direction):
    return passed_along(tensor, "row", direction)


def row_sums(term_fn, shard_rows):
    return lax.psum_scatter(
        term_fn(jnp.int32(0), shard_rows * lax.axis_size("env")),
        "env",
        scatter_dimension=0,
        tiled=True,
    )


def shards(corner, top_edge, half_system, values, cotangent, parity):
    shard_rows = top_edge.shape[2]
    row_start = lax.axis_index("env") * shard_rows
    charges = jnp.repeat(parity[0, 0], BLK, axis=1)
    corner_mask = charges[0][:, None] == charges[1][None, :]
    out_mask = charges[2][:, None] == charges[3][None, :]
    near_corner = side_column(corner[0, 0], 1)
    near_corner = jnp.where(corner_mask, near_corner, jnp.zeros_like(near_corner))
    lower_half = side_row(half_system[0, 0], -1).reshape(shard_rows, CHI, HALF)
    absorbed = jnp.einsum(
        "ab,iak->ibk", near_corner, lower_half, preferred_element_type=jnp.float32
    )
    absorbed = absorbed.astype(jnp.bfloat16).reshape(shard_rows, CHI * HALF)
    gathered = lax.all_to_all(absorbed, "env", split_axis=1, concat_axis=0, tiled=True)
    edge_mat = top_edge[0, 0].reshape(shard_rows * HALF, CHI)
    weight = values[0, 0] ** (-0.5)
    grad_new = jnp.where(
        out_mask, weight[:, None] * cotangent[0, 0].astype(jnp.float32), 0.0
    ).astype(jnp.bfloat16)
    grad_edge = jnp.einsum("ij,ie->je", gathered, grad_new, preferred_element_type=jnp.float32)
    grad_edge = grad_edge.astype(jnp.bfloat16).reshape(shard_rows, HALF * CHI)
    grad_full = jnp.einsum("ie,je->ij", grad_new, edge_mat, preferred_element_type=jnp.float32)
    totals = lax.psum(jnp.sum(gathered * grad_full, axis=1), "env")
    pair_sums = lax.dynamic_slice_in_dim(totals, row_start, shard_rows, 0)
    own_values = lax.dynamic_slice_in_dim(values[0, 0], row_start, shard_rows, 0)
    grad_values = -0.5 * pair_sums / own_values
    grad_back = lax.all_to_all(
        grad_full.astype(jnp.bfloat16), "env", split_axis=0, concat_axis=1, tiled=True
    )
    grad_back = grad_back.reshape(shard_rows, CHI, HALF)
    grad_half = jnp.einsum(
        "ab,ibk->iak", near_corner, grad_back, preferred_element_type=jnp.float32
    )
    grad_half = grad_half.astype(jnp.bfloat16).reshape(shard_rows, CHI * HALF)

    def corner_terms(offset, length):
        return jnp.einsum("iak,ibk->ab", lower_half, grad_back, preferred_element_type=jnp.float32)

    summed = row_sums(corner_terms, shard_rows)
    own_mask = lax.dynamic_slice_in_dim(corner_mask, row_start, shard_rows, 0)
    grad_corner = jnp.where(own_mask, summed, 0.0).astype(jnp.bfloat16)
    grad_corner = side_column(grad_corner, -1)
    grad_half = side_row(grad_half, 1)
    return (
        grad_corner[None, None],
        grad_edge[None, None],
        grad_half[None, None],
        grad_values[None, None],
    )


def solution(mesh):
    placed = (
        P("row", "col", None, None),
        P("row", "col", "env", None),
        P("row", "col", "env", None),
        P("row", "col", None),
        P("row", "col", None, None),
        P("row", "col", None, None),
    )
    return jax.shard_map(
        shards,
        mesh=mesh,
        in_specs=placed,
        out_specs=(
            P("row", "col", "env", None),
            P("row", "col", "env", None),
            P("row", "col", "env", None),
            P("row", "col", "env"),
        ),
        check_vma=False,
    )
```

profile of v0, /device:TPU:1, one launch (start us, length us, event | category | flops | bytes accessed | tf_op | source)
XLA Modules:
  0.0 466.5 jit_solution(613649358978796552)
XLA Ops:
  7.2 0.0 copy-start.2
  7.2 3.3 collective-permute-start
  10.5 3.9 copy.29
  14.4 1.2 collective-permute-start.2
  15.6 0.0 copy-done.2
  15.6 0.1 broadcast_bitcast_fusion.2
  15.7 34.8 %collective-permute-done = bf16[32,32768]{1,0:T(8,128)(2,1)S(1)} collective-permute-done((bf16[32,32768]{1,0:T(8,128)(2,1)}, bf16[32,32768]{1,0:T(8,128)(2,1)S(1)}, u32[]{:S(2)}, u32[]{:S(2)}) %collective-permute-start) | collective-permute-done | bytes 2097184 | tf_op jit(solution)/shard_map/ppermute | solution.py:13
  50.5 7.9 %reshape.146 = bf16[32,1024,32]{2,1,0:T(8,128)(2,1)} reshape(bf16[32,32768]{1,0:T(8,128)(2,1)S(1)} %collective-permute-done) | data formatting | bytes 4194304 | tf_op jit(solution)/shard_map/reshape | solution.py:41
  58.4 6.7 %copy.31 = bf16[32,1024,32]{1,2,0:T(8,128)(2,1)S(1)} copy(bf16[32,1024,32]{2,1,0:T(8,128)(2,1)} %reshape.146) | data formatting | bytes 4194304 | tf_op jit(solution)/shard_map/reshape | solution.py:41
  65.1 0.0 collective-permute-done.2
  65.1 4.0 fusion.6
  69.2 0.3 convert_bitcast_fusion.1
  69.5 5.9 %copy.32 = bf16[32,1024,32]{2,1,0:T(8,128)(2,1)} copy(bf16[32,1024,32]{1,2,0:T(8,128)(2,1)S(1)} %convert_bitcast_fusion.1) | data formatting | bytes 4194304 | tf_op jit(solution)/shard_map/convert_element_type | solution.py:45
  75.4 11.3 %all_to_all.29 = bf16[32,32,1024]{2,1,0:T(8,128)(2,1)S(1)} reshape(bf16[32,1024,32]{2,1,0:T(8,128)(2,1)} %copy.32) | data formatting | bytes 4194304 | tf_op jit(solution)/shard_map/all_to_all | solution.py:46
  86.7 2.5 copy.33
  89.2 0.0 copy-start
  89.2 11.3 %all-to-all-start.1 = ((bf16[32,32,1024]{2,0,1:T(8,128)(2,1)}), bf16[32,32,1024]{2,0,1:T(8,128)(2,1)}, u32[]{:S(2)}, u32[]{:S(2)}) async-start(bf16[32,32,1024]{2,0,1:T(8,128)(2,1)} %copy.33), calls=%async_computation.1 | async-start | bytes 4194304 | tf_op jit(solution)/shard_map/all_to_all | solution.py:46
  100.5 0.0 copy-start.1
  100.5 0.0 reduce-scatter.4.cloned.1.call-start
  100.6 0.0 copy-done
  100.6 2.3 reshape_squeeze.3
  102.9 0.0 copy-done.1
  102.9 0.1 broadcast_bitcast_fusion
  103.0 27.8 %all-to-all-done.1 = bf16[32,32,1024]{2,0,1:T(8,128)(2,1)} async-done(((bf16[32,32,1024]{2,0,1:T(8,128)(2,1)}), bf16[32,32,1024]{2,0,1:T(8,128)(2,1)}, u32[]{:S(2)}, u32[]{:S(2)}) %all-to-all-start.1) | async-done | bytes 2097184 | tf_op jit(solution)/shard_map/all_to_all | solution.py:46
  130.8 5.3 %multiply_reduce_fusion = (f32[1024]{0:T(1024)S(1)}, bf16[1024,1024]{1,0:T(8,128)(2,1)S(1)}) fusion(bf16[32,32,1024]{2,0,1:T(8,128)(2,1)} %all-to-all-done.1, bf16[1024,1024]{1,0:T(8,128)(2,1)} %reshape_squeeze.3, bf16[1,1,1024,1024]{3,2,1,0:T(8,128)(2,1)} %param.10, f32[1024]{0:T(1024)S(1)} %bitcast.71, s32[1024]{0:T(1024)S(1)} %get-tuple-element.23, ...), kind=kOutput, calls=%fused_computation | convolution fusion | flops 2156919808 | bytes 8404992 | tf_op jit(solution)/shard_map/ie,je->ij/dot_general | solution.py:54
  136.1 42.2 %all_to_all.35 = bf16[32,32,1024]{2,1,0:T(8,128)(2,1)S(1)} all-to-all(bf16[32,32,1024]{2,1,0:T(8,128)(2,1)S(1)} %bitcast.69), channel_id=1, replica_groups=mesh['row'=4,'col'=2,'env'=32] {'env'}, dimensions={0} | all-to-all | bytes 4194304 | tf_op jit(solution)/shard_map/all_to_all | solution.py:59
  178.3 1.2 copy.26
  179.5 7.9 %reshape.145 = bf16[32,1024,32]{2,1,0:T(8,128)(2,1)} reshape(bf16[32,32,1024]{2,1,0:T(8,128)(2,1)S(1)} %copy.26) | data formatting | bytes 4194304 | tf_op jit(solution)/shard_map/reshape | solution.py:62
  187.4 15.1 %convolution_bitcast_fusion = f32[1024,1024]{0,1:T(8,128)} fusion(bf16[32,1024,32]{2,1,0:T(8,128)(2,1)} %reshape.145, bf16[32,1024,32]{2,1,0:T(8,128)(2,1)} %reshape.146), kind=kOutput, calls=%fused_computation.2 | convolution fusion | flops 2147483648 | bytes 8388608 | tf_op jit(solution)/shard_map/iak,ibk->ab/dot_general | solution.py:69
  202.5 5.4 %copy.44 = f32[1024,1024]{1,0:T(8,128)} copy(f32[1024,1024]{0,1:T(8,128)} %convolution_bitcast_fusion) | data formatting | bytes 8388608
  207.8 0.0 reduce-scatter.4.cloned.1.call-update
  207.9 7.0 %convert_bitcast_fusion = bf16[32,1024,32]{1,2,0:T(8,128)(2,1)S(1)} fusion(bf16[32,1024,32]{2,1,0:T(8,128)(2,1)} %reshape.145, bf16[1024,1024]{0,1:T(8,128)(2,1)} %collective-permute-done.2, s32[1024]{0:T(1024)S(1)} %get-tuple-element.26, s32[1024]{0:T(1024)S(1)} %get-tuple-element.25), kind=kOutput, calls=%fused_computation.6 | convolution fusion | flops 2150629376 | bytes 6299648 | tf_op jit(solution)/shard_map/ab,ibk->iak/dot_general | solution.py:63
  214.9 5.9 %copy.36 = bf16[32,1024,32]{2,1,0:T(8,128)(2,1)} copy(bf16[32,1024,32]{1,2,0:T(8,128)(2,1)S(1)} %convert_bitcast_fusion) | data formatting | bytes 4194304 | tf_op jit(solution)/shard_map/convert_element_type | solution.py:66
  220.7 10.5 %reshape.147 = bf16[32,32768]{1,0:T(8,128)(2,1)S(1)} reshape(bf16[32,1024,32]{2,1,0:T(8,128)(2,1)} %copy.36) | data formatting | bytes 4194304 | tf_op jit(solution)/shard_map/reshape | solution.py:66
  231.3 21.1 %collective-permute-start.3 = (bf16[32,32768]{1,0:T(8,128)(2,1)S(1)}, bf16[32,32768]{1,0:T(8,128)(2,1)}, u32[]{:S(2)}, u32[]{:S(2)}) collective-permute-start(bf16[32,32768]{1,0:T(8,128)(2,1)S(1)} %reshape.147), channel_id=1, source_target_pairs={{0,64},{64,128},{128,192},{192,0},{1,65},{65,129},{129,193},{193,1... | collective-permute-start | bytes 6291464 | tf_op jit(solution)/shard_map/ppermute | solution.py:13
  252.4 0.7 broadcast_compare_fusion
  253.1 6.3 %convolution_convert_fusion = bf16[1024,1024]{1,0:T(8,128)(2,1)} fusion(bf16[1024,1024]{1,0:T(8,128)(2,1)} %bitcast.22, bf16[1,1,1024,1024]{3,2,1,0:T(8,128)(2,1)} %param.10, f32[1024]{0:T(1024)S(1)} %bitcast.72, s32[1024]{0:T(1024)S(1)} %get-tuple-element.23, s32[1024]{0:T(1024)S(1)} %get-tuple-element.24), kind=kOutput, calls=%fused_computation.9 | convolution fusion | flops 2153775104 | bytes 6303744 | tf_op jit(solution)/shard_map/ij,ie->je/dot_general | solution.py:52
  259.3 4.2 broadcast_in_dim_reshape.3
  263.5 59.3 %psum.7 = f32[1024]{0:T(1024)S(1)} all-reduce(f32[1024]{0:T(1024)S(1)} %get-tuple-element.16), channel_id=1, replica_groups=mesh['row'=4,'col'=2,'env'=32] {'env'}, use_global_device_ids=true, to_apply=%region_2.3 | all-reduce | flops 1024 | bytes 8192 | tf_op jit(solution)/shard_map/psum | solution.py:55
  322.8 124.9 %reduce-scatter.4.cloned.1.call-done = f32[32,1024]{1,0:T(8,128)} async-done(((f32[1024,1024]{1,0:T(8,128)}), f32[32,1024]{1,0:T(8,128)}) %reduce-scatter.4.cloned.1.call-update) | async-done | bytes 131088
  447.8 1.1 copy.45
  448.8 0.2 select_convert_fusion.1
  449.1 2.8 collective-permute-start.1
  451.8 0.6 fusion.10
  452.4 0.0 collective-permute-done.3
  452.4 3.4 collective-permute-done.1
  455.9 0.8 copy.37
  456.6 3.0 copy.47
  (2 shorter events, 0.0 us)
Async XLA Ops:
  7.2 8.4 %copy-start.2 = (s32[1,1,4,8]{3,2,1,0:T(4,128)S(1)}, s32[1,1,4,8]{3,2,1,0:T(4,128)}, u32[]{:S(2)}) copy-start(s32[1,1,4,8]{3,2,1,0:T(4,128)} %param.11) | copy-start | bytes 388
  7.2 43.3 %collective-permute-start = (bf16[32,32768]{1,0:T(8,128)(2,1)}, bf16[32,32768]{1,0:T(8,128)(2,1)S(1)}, u32[]{:S(2)}, u32[]{:S(2)}) collective-permute-start(bf16[32,32768]{1,0:T(8,128)(2,1)} %bitcast.73), channel_id=1, source_target_pairs={{0,192},{64,0},{128,64},{192,128},{1,193},{65,1},{129,65},{193,129... | collective-permute-start | bytes 6291464 | tf_op jit(solution)/shard_map/ppermute | solution.py:13
  14.4 50.7 %collective-permute-start.2 = (bf16[1024,1024]{0,1:T(8,128)(2,1)}, bf16[1024,1024]{0,1:T(8,128)(2,1)}, u32[]{:S(2)}, u32[]{:S(2)}) collective-permute-start(bf16[1024,1024]{0,1:T(8,128)(2,1)} %bitcast.68), channel_id=1, source_target_pairs={{0,32},{32,0},{1,33},{33,1},{2,34},{34,2},{3,35},{35,3},{4,36},{36... | collective-permute-start | bytes 6291464 | tf_op jit(solution)/shard_map/ppermute | solution.py:13
  89.2 11.4 %copy-start = (bf16[1,1,32,32768]{3,2,1,0:T(8,128)(2,1)S(1)}, bf16[1,1,32,32768]{3,2,1,0:T(8,128)(2,1)}, u32[]{:S(2)}) copy-start(bf16[1,1,32,32768]{3,2,1,0:T(8,128)(2,1)} %param.7) | copy-start | bytes 6291460
  89.2 41.6 %all-to-all-start.1 = ((bf16[32,32,1024]{2,0,1:T(8,128)(2,1)}), bf16[32,32,1024]{2,0,1:T(8,128)(2,1)}, u32[]{:S(2)}, u32[]{:S(2)}) async-start(bf16[32,32,1024]{2,0,1:T(8,128)(2,1)} %copy.33), calls=%async_computation.1 | async-start | bytes 4194304 | tf_op jit(solution)/shard_map/all_to_all | solution.py:46
  100.5 2.4 copy-start.1
  100.5 347.2 %reduce-scatter.4.cloned.1.call-start = ((), (), s32[]{:S(2)}) async-start(), calls=%async_computation.3 | async-start | bytes 4325376
  231.3 221.2 %collective-permute-start.3 = (bf16[32,32768]{1,0:T(8,128)(2,1)S(1)}, bf16[32,32768]{1,0:T(8,128)(2,1)}, u32[]{:S(2)}, u32[]{:S(2)}) collective-permute-start(bf16[32,32768]{1,0:T(8,128)(2,1)S(1)} %reshape.147), channel_id=1, source_target_pairs={{0,64},{64,128},{128,192},{192,0},{1,65},{65,129},{129,193},{193,1... | collective-permute-start | bytes 6291464 | tf_op jit(solution)/shard_map/ppermute | solution.py:13
  449.1 6.8 %collective-permute-start.1 = (bf16[32,1024]{0,1:T(8,128)(2,1)S(1)}, bf16[32,1024]{0,1:T(8,128)(2,1)S(1)}, u32[]{:S(2)}, u32[]{:S(2)}) collective-permute-start(bf16[32,1024]{0,1:T(8,128)(2,1)S(1)} %select_convert_fusion.1), channel_id=1, source_target_pairs={{0,32},{32,0},{1,33},{33,1},{2,34},{34,2},{3,35},{35,3},{4,36},{36... | collective-permute-start | bytes 196616 | tf_op jit(solution)/shard_map/ppermute | solution.py:13
Sparse Core Ops, SparseCore 0:
  208.0 239.7 reduce-scatter.3
where the time goes:
time: 473 us; the launch traced here: 467 us
  waiting for transfers between devices  191 us (40%)
  blocking collectives  102 us (22%)
  local copies, waits for them, and re-layouts  80.7 us (17%)
  starting transfers between devices  39.8 us (8%)
  matrix products  37.7 us (8%)
  between operations  14.2 us (3%)
    unnamed x2, waiting for transfers between devices  125 us
    psum x1, blocking collectives, shards(): totals = lax.psum(jnp.sum(gathered * grad_full, axis=1), 'env')  59.3 us
    all_to_all x1, blocking collectives, shards(): lax.all_to_all(grad_full.astype(jnp.bfloat16), 'env', split_axis=0, conca...  42.2 us
    ppermute x4, waiting for transfers between devices, passed_along(): return lax.ppermute(x, axis, [(i, (i + by) % size) for i in range(size)])  38.3 us
    ppermute x4, starting transfers between devices, passed_along(): return lax.ppermute(x, axis, [(i, (i + by) % size) for i in range(size)])  28.4 us
    all_to_all x1, waiting for transfers between devices, shards(): lax.all_to_all(absorbed, 'env', split_axis=1, concat_axis=0, tiled=True)  27.8 us
    dot_general x1, matrix products, corner_terms(): jnp.einsum('iak,ibk->ab', lower_half, grad_back, preferred_element_type=j...  15.1 us
    reshape x2, local copies, waits for them, and re-layouts, shards(): lower_half = side_row(half_system[0, 0], -1).reshape(shard_rows, CHI, HALF)  14.6 us
  transfers between devices with their start and end apart: 6, of which 4 were waited for; matrix products, arithmetic and copies ran while one was open for 12% of the time, Pallas kernels for 0%

commit v1 on v0

v1 whole, which is shorter than its diff:
```python
import functools

import jax
import jax.numpy as jnp
from jax import lax
from jax.experimental import pallas as pl
from jax.experimental.pallas import tpu as pltpu
from jax.sharding import PartitionSpec as P

CHI = 1024
HALF = 32
BLK = 128
NBLK = CHI // BLK
LANE = 128
SUB = 4
GRP = CHI // SUB
NX, NZ = 4, 8
ROWS_A = 32
QN = 4
QW = CHI // QN
KQ = HALF // QN
MESH = pl.DeviceIdType.MESH
F32 = jnp.float32
BF16 = jnp.bfloat16


def tile_mix(tiles):
    lane = lax.broadcasted_iota(jnp.int32, tiles[0].shape, 1)
    low = lane < 64
    even = (lane // 32) % 2 == 0
    roll = lambda t, by: pltpu.roll(t, by, 1)
    x0, x1, x2, x3 = tiles
    y0 = jnp.where(low, x0, roll(x2, 64))
    y2 = jnp.where(low, roll(x0, 64), x2)
    y1 = jnp.where(low, x1, roll(x3, 64))
    y3 = jnp.where(low, roll(x1, 64), x3)
    z0 = jnp.where(even, y0, roll(y1, 32))
    z1 = jnp.where(even, roll(y0, 96), y1)
    z2 = jnp.where(even, y2, roll(y3, 32))
    z3 = jnp.where(even, roll(y2, 96), y3)
    return z0, z1, z2, z3


def dot_nn(a, b):
    return lax.dot_general(a, b, (((1,), (0,)), ((), ())), preferred_element_type=F32)


def dot_nt(a, b):
    return lax.dot_general(a, b, (((1,), (1,)), ((), ())), preferred_element_type=F32)


def dot_tn(a, b):
    return lax.dot_general(a, b, (((0,), (0,)), ((), ())), preferred_element_type=F32)


def at(start, size):
    return pl.ds(pl.multiple_of(start, size), size)


def loop(n, body):
    lax.fori_loop(0, n, lambda i, c: (body(i), c)[1], 0)


def kernel(
    nr, nc, ne,
    corner, te, lh, gn_in, ch, vals,
    gc_out, ge_out, gh_out, gv_out,
    TE, GN, LHB, CR, CHR, GFS, R, AS, G, NCP, LHM, GFM, S, LM, F, GCB, P1, P1S, P2, PSA, PSS, PSR,
    te_sem, in_sem, out_sem, cn_send, cn_recv, ch_send, ch_recv,
    gf_send, gf_recv, ab_send, ab_recv, p1_send, p1_recv, p2_send, p2_recv, ps_send, ps_recv,
):
    r, c, e = lax.axis_index("row"), lax.axis_index("col"), lax.axis_index("env")
    rp, rm = lax.rem(r + 1, nr), lax.rem(r + nr - 1, nr)
    cp, cm = lax.rem(c + 1, nc), lax.rem(c + nc - 1, nc)
    x, z = e // NZ, lax.rem(e, NZ)

    def dev(row, col, env):
        return {"row": row, "col": col, "env": env}

    def remote(src, dst, send, recv, where):
        return pltpu.make_async_remote_copy(
            src_ref=src, dst_ref=dst, send_sem=send, recv_sem=recv, device_id=where, device_id_type=MESH
        )

    barrier = pltpu.get_barrier_semaphore()

    def greet(where):
        pl.semaphore_signal(barrier, inc=1, device_id=where, device_id_type=MESH)

    def greet_env(s):
        greet(dev(rp, c, s))
        greet(dev(rm, c, s))

    def greet_z(s):
        greet(dev(rp, cp, x * NZ + s))
        greet(dev(rm, cm, x * NZ + s))

    def greet_x(s):
        greet(dev(r, c, lax.rem(x + 1 + s, NX) * NZ + z))

    loop(ne, greet_env)
    loop(NZ, greet_z)
    loop(NX - 1, greet_x)

    gn_copy = pltpu.make_async_copy(gn_in, GN, in_sem.at[0])
    gn_copy.start()

    def load_edge(k):
        pltpu.make_async_copy(
            te.at[:, at(k * CHI, CHI)], TE.at[at(k * ROWS_A, ROWS_A), :], te_sem.at[k // KQ]
        ).start()

    loop(HALF, load_edge)
    lh_copy = pltpu.make_async_copy(lh, LHB, in_sem.at[1])
    lh_copy.start()
    gn_copy.wait()

    pl.semaphore_wait(barrier, 2 * ne + 2 * NZ + NX - 1)

    remote(ch, CHR, ch_send, ch_recv, dev(rp, c, e)).start()

    def send_corner(g):
        rows = at(g * BLK, BLK)
        remote(corner.at[rows, :], CR.at[rows, :], cn_send, cn_recv.at[g], dev(rp, cp, e)).start()

    def edge_chunk(q):
        cols = at(q * QW, QW)
        whole = TE.at[cols, :]
        pltpu.make_async_copy(whole, whole, te_sem.at[q]).wait()

        def rows_of(m):
            rows = at(m * 256, 256)
            GFS[rows, cols] = dot_nt(GN[rows, :], TE[cols, :]).astype(BF16)

        loop(CHI // 256, rows_of)

        def send(j):
            s = lax.rem(e + j, ne)
            remote(
                GFS.at[at(s * ROWS_A, ROWS_A), cols], R.at[at(e * ROWS_A, ROWS_A), cols],
                gf_send.at[q], gf_recv.at[q], dev(rp, c, s),
            ).start()

        loop(ne, send)

    loop(NBLK, send_corner)
    loop(QN, edge_chunk)

    lh_copy.wait()

    def spread(g):
        for u in range(8):
            S[at((g * 8 + u) * ROWS_A, ROWS_A), :] = LHB[:, at((g * 8 + u) * LANE, LANE)].astype(F32)

    loop(GRP // 8, spread)

    def turn(i):
        t = S[pl.ds(i, GRP, stride=ROWS_A), :].T
        for s in range(SUB):
            for h in range(GRP // LANE):
                LM[s * (GRP // LANE) + h, pl.ds(i, HALF, stride=ROWS_A), :] = t[
                    s * HALF:(s + 1) * HALF, h * LANE:(h + 1) * LANE]

    loop(ROWS_A, turn)

    def narrow(k):
        rows = at(k * ROWS_A, ROWS_A)
        for t in range(CHI // LANE):
            LHM[rows, t * LANE:(t + 1) * LANE] = LM[t, rows, :].astype(BF16)

    loop(HALF, narrow)

    remote(CHR, CHR, ch_send, ch_recv, dev(rp, c, e)).wait_recv()

    def corner_rows(g):
        rows = at(g * BLK, BLK)
        part = CR.at[rows, :]
        remote(part, part, cn_send, cn_recv.at[g], dev(rp, cp, e)).wait_recv()
        charge = CHR[0:1, rows]
        for t in range(CHI // LANE):
            lanes = slice(t * LANE, (t + 1) * LANE)
            same = charge == CHR[1:2, lanes]
            F[t, rows, :] = jnp.where(same, CR[rows, lanes].astype(F32), 0.0)
            for s in range(SUB):
                NCP[at(s * GRP + g * (BLK // SUB), BLK // SUB), lanes] = F[
                    t, pl.ds(g * BLK + s, BLK // SUB, stride=SUB), :].astype(BF16)

    loop(NBLK, corner_rows)

    def absorb_chunk(q):
        cols = at(q * QW, QW)

        def columns_of(n):
            t = dot_nn(LHM[cols, :], NCP[:, at(n * 256, 256)])
            for k2 in range(KQ // 4):
                for d2 in range(2):
                    mixed = tile_mix([
                        t[(k2 * 4 + k4) * ROWS_A:(k2 * 4 + k4 + 1) * ROWS_A, d2 * LANE:(d2 + 1) * LANE]
                        for k4 in range(4)])
                    for d4 in range(4):
                        AS[at(((n * 2 + d2) * 4 + d4) * ROWS_A, ROWS_A), at(q * QW + k2 * LANE, LANE)] = (
                            mixed[d4].astype(BF16))

        loop(CHI // 256, columns_of)

        def send(j):
            s = lax.rem(e + j, ne)
            remote(
                AS.at[at(s * ROWS_A, ROWS_A), cols], G.at[at(e * ROWS_A, ROWS_A), cols],
                ab_send.at[q], ab_recv.at[q], dev(rm, c, s),
            ).start()

        loop(ne, send)

    loop(QN, absorb_chunk)

    PSA[...] = jnp.zeros_like(PSA)

    def half_chunk(q):
        cols = at(q * QW, QW)
        whole = R.at[:, cols]
        remote(whole, whole, gf_send.at[q], gf_recv.at[q], dev(rp, c, e)).wait_recv()

        def regroup(d):
            for k2 in range(KQ // 4):
                lanes = at(q * QW + k2 * LANE, LANE)
                tiles = []
                total = PSA[...]
                for d4 in range(4):
                    rows = at((d * 4 + d4) * ROWS_A, ROWS_A)
                    tile = R[rows, lanes].astype(F32)
                    total = total + tile * AS[rows, lanes].astype(F32)
                    tiles.append(tile)
                PSA[...] = total
                mixed = tile_mix(tiles)
                for k4 in range(4):
                    GFM[at((q * KQ + k2 * 4 + k4) * ROWS_A, ROWS_A), at(d * LANE, LANE)] = mixed[k4].astype(BF16)

        loop(CHI // LANE, regroup)

        def half_cols(n):
            t = dot_nt(GFM[cols, :], NCP[at(n * 256, 256), :])
            for h in range(2):
                LM[n * 2 + h, cols, :] = t[:, h * LANE:(h + 1) * LANE]

        loop(CHI // 256, half_cols)

    loop(QN, half_chunk)

    PSS[...] = jnp.broadcast_to(jnp.sum(PSA[...], axis=1, keepdims=True), (ROWS_A, LANE))
    ps_copy = remote(PSS, PSR, ps_send, ps_recv, dev(rm, c, e))
    ps_copy.start()

    def corner_part(s):
        t = dot_tn(LHM[:, at(s * GRP, GRP)], GFM[...])
        for g in range(NBLK):
            for h in range(CHI // LANE):
                same = CHR[0:1, g * BLK:(g + 1) * BLK] == CHR[1:2, h * LANE:(h + 1) * LANE]
                part = t[g * (BLK // SUB):(g + 1) * (BLK // SUB), h * LANE:(h + 1) * LANE]
                F[h, pl.ds(g * BLK + s, BLK // SUB, stride=SUB), :] = jnp.where(same, part, 0.0)

    loop(SUB, corner_part)

    def corner_narrow(g):
        rows = at(g * 32, 32)
        for t in range(CHI // LANE):
            GCB[rows, t * LANE:(t + 1) * LANE] = F[t, rows, :].astype(BF16)

    loop(CHI // 32, corner_narrow)
    span = CHI // NX

    def send_x(j):
        to = lax.rem(x + 1 + j, NX)
        remote(
            GCB.at[at(to * span, span), :], P1.at[j], p1_send, p1_recv, dev(r, c, to * NZ + z)
        ).start()

    loop(NX - 1, send_x)

    def turn_back(i):
        t = jnp.concatenate([
            jnp.concatenate([
                LM[s * (GRP // LANE) + h, pl.ds(i, HALF, stride=ROWS_A), :] for h in range(GRP // LANE)
            ], axis=1) for s in range(SUB)], axis=0)
        S[pl.ds(i, GRP, stride=ROWS_A), :] = t.T

    loop(ROWS_A, turn_back)

    def gather(g):
        for u in range(8):
            LHB[:, at((g * 8 + u) * LANE, LANE)] = S[at((g * 8 + u) * ROWS_A, ROWS_A), :].astype(BF16)

    loop(GRP // 8, gather)
    gh_copy = pltpu.make_async_copy(LHB, gh_out, in_sem.at[1])
    gh_copy.start()

    remote(P1, P1, p1_send, p1_recv, dev(r, c, e)).wait_recv()

    def sum_x(g):
        rows = at(g * 32, 32)
        for t in range(CHI // LANE):
            lanes = slice(t * LANE, (t + 1) * LANE)
            total = F[t, at(x * span + g * 32, 32), :]
            for j in range(NX - 1):
                total = total + P1[j, rows, lanes].astype(F32)
            P1S[rows, lanes] = total.astype(BF16)

    loop(span // 32, sum_x)

    def send_z(j):
        to = lax.rem(z + j, NZ)
        remote(
            P1S.at[at(to * ROWS_A, ROWS_A), :], P2.at[at(z * ROWS_A, ROWS_A), :],
            p2_send, p2_recv, dev(rm, cm, x * NZ + to),
        ).start()

    loop(NZ, send_z)

    def edge_grad(q):
        cols = at(q * QW, QW)
        whole = G.at[:, cols]
        remote(whole, whole, ab_send.at[q], ab_recv.at[q], dev(rm, c, e)).wait_recv()
        TE[cols, :] = dot_tn(G[:, cols], GN[...]).astype(BF16)

        def store(j):
            k = q * KQ + j
            pltpu.make_async_copy(
                TE.at[at(k * ROWS_A, ROWS_A), :], ge_out.at[:, at(k * CHI, CHI)], out_sem
            ).start()

        loop(KQ, store)

    loop(QN, edge_grad)

    remote(P2, P2, p2_send, p2_recv, dev(rm, cm, e)).wait_recv()
    for t in range(CHI // LANE):
        lanes = slice(t * LANE, (t + 1) * LANE)
        total = P2[0:ROWS_A, lanes].astype(F32)
        for j in range(1, NZ):
            total = total + P2[j * ROWS_A:(j + 1) * ROWS_A, lanes].astype(F32)
        gc_out[:, lanes] = total.astype(BF16)

    ps_copy.wait_recv()
    own = lax.broadcasted_iota(jnp.int32, (ROWS_A, LANE), 0) == lax.broadcasted_iota(jnp.int32, (ROWS_A, LANE), 1)
    sums = jnp.sum(jnp.where(own, PSR[...], 0.0), axis=0, keepdims=True)
    gv_out[...] = -0.5 * sums[:, :ROWS_A] / vals[...]

    ps_copy.wait_send()
    remote(ch, CHR, ch_send, ch_recv, dev(rp, c, e)).wait_send()
    remote(CR, CR, cn_send, cn_recv.at[0], dev(rp, cp, e)).wait_send()
    for q in range(QN):
        part = GFS.at[:, q * QW:(q + 1) * QW]
        remote(part, part, gf_send.at[q], gf_recv.at[q], dev(rp, c, e)).wait_send()
        part = AS.at[:, q * QW:(q + 1) * QW]
        remote(part, part, ab_send.at[q], ab_recv.at[q], dev(rm, c, e)).wait_send()
    remote(P1, P1, p1_send, p1_recv, dev(r, c, e)).wait_send()
    remote(P1S, P1S, p2_send, p2_recv, dev(rm, cm, e)).wait_send()
    gh_copy.wait()
    pltpu.make_async_copy(TE, TE, out_sem).wait()


def absorb_backward(sizes, corner, te, lh, gn, ch, vals):
    nr, nc, ne = sizes
    hbm = pl.BlockSpec(memory_space=pl.ANY)
    vmem = pl.BlockSpec(memory_space=pltpu.VMEM)
    dma = pltpu.SemaphoreType.DMA
    square = pltpu.VMEM((CHI, CHI), BF16)
    tiles = pltpu.VMEM((CHI // LANE, CHI, LANE), F32)
    scratch = [
        square, square, pltpu.VMEM((ROWS_A, CHI * HALF), BF16), square, pltpu.VMEM((8, CHI), jnp.int32),
        square, square, square, square, square, square, square,
        pltpu.VMEM((GRP * ROWS_A, LANE), F32), tiles, tiles, square,
        pltpu.VMEM((NX - 1, CHI // NX, CHI), BF16), pltpu.VMEM((CHI // NX, CHI), BF16),
        pltpu.VMEM((NZ * ROWS_A, CHI), BF16),
        pltpu.VMEM((ROWS_A, LANE), F32), pltpu.VMEM((ROWS_A, LANE), F32), pltpu.VMEM((ROWS_A, LANE), F32),
        dma((QN,)), dma((2,)), dma, dma, dma((NBLK,)), dma, dma,
        dma((QN,)), dma((QN,)), dma((QN,)), dma((QN,)), dma, dma, dma, dma, dma, dma,
    ]
    return pl.pallas_call(
        functools.partial(kernel, nr, nc, ne),
        out_shape=(
            jax.ShapeDtypeStruct((ROWS_A, CHI), BF16),
            jax.ShapeDtypeStruct((ROWS_A, HALF * CHI), BF16),
            jax.ShapeDtypeStruct((ROWS_A, CHI * HALF), BF16),
            jax.ShapeDtypeStruct((1, ROWS_A), F32),
        ),
        in_specs=[hbm, hbm, hbm, hbm, hbm, vmem],
        out_specs=(vmem, hbm, hbm, vmem),
        scratch_shapes=scratch,
        compiler_params=pltpu.CompilerParams(
            collective_id=0, has_side_effects=True, vmem_limit_bytes=60 * 1024 * 1024
        ),
    )(corner, te, lh, gn, ch, vals)


def shards(sizes, corner, top_edge, half_system, values, cotangent, parity):
    rows = top_edge.shape[2]
    charges = jnp.repeat(parity[0, 0], BLK, axis=1)
    out_mask = charges[2][:, None] == charges[3][None, :]
    weight = values[0, 0] ** (-0.5)
    grad_new = jnp.where(out_mask, weight[:, None] * cotangent[0, 0].astype(F32), 0.0).astype(BF16)
    ch = jnp.concatenate([charges, charges], axis=0)
    own = lax.dynamic_slice_in_dim(values[0, 0], lax.axis_index("env") * rows, rows, 0)[None, :]
    gc, ge, gh, gv = absorb_backward(
        sizes, corner[0, 0], top_edge[0, 0], half_system[0, 0], grad_new, ch, own
    )
    return gc[None, None], ge[None, None], gh[None, None], gv[None]


def solution(mesh):
    placed = (
        P("row", "col", None, None),
        P("row", "col", "env", None),
        P("row", "col", "env", None),
        P("row", "col", None),
        P("row", "col", None, None),
        P("row", "col", None, None),
    )
    sizes = (mesh.shape["row"], mesh.shape["col"], mesh.shape["env"])
    return jax.shard_map(
        functools.partial(shards, sizes),
        mesh=mesh,
        in_specs=placed,
        out_specs=(
            P("row", "col", "env", None),
            P("row", "col", "env", None),
            P("row", "col", "env", None),
            P("row", "col", "env"),
        ),
        check_vma=False,
    )
```

time: 473 us -> 150 us (0.32); the launches traced: 467 us -> 149 us
  waiting for transfers between devices: 191 us -> 0 us
  Pallas kernels: 0 us -> 135 us
  blocking collectives: 102 us -> 0 us
  local copies, waits for them, and re-layouts: 80.7 us -> 10 us
  starting transfers between devices: 39.8 us -> 0 us
  matrix products: 37.7 us -> 0 us
  between operations: 14.2 us -> 0.65 us
    pallas_call x0 -> x1, Pallas kernels: none -> 135 us  [absorb_backward(): pl.pallas_call(functools.partial(kernel, nr, nc, ne), out_shape=(jax.Shap...]
    unnamed x2 -> x0, waiting for transfers between devices: 125 us -> none
    psum x1 -> x0, blocking collectives: 59.3 us -> none  [shards(): totals = lax.psum(jnp.sum(gathered * grad_full, axis=1), 'env')]
    all_to_all x1 -> x0, blocking collectives: 42.2 us -> none  [shards(): lax.all_to_all(grad_full.astype(jnp.bfloat16), 'env', split_axis=0, conca...]
    ppermute x4 -> x0, waiting for transfers between devices: 38.3 us -> none  [passed_along(): return lax.ppermute(x, axis, [(i, (i + by) % size) for i in range(size)])]
    dot_general x4 -> x0, matrix products: 33.7 us -> none  [the longest x1 15.1 us: corner_terms(): jnp.einsum('iak,ibk->ab', lower_half, grad_back, preferred_element_type=j...]
    reshape x4 -> x0, local copies, waits for them, and re-layouts: 33.1 us -> none  [the longest x2 14.6 us: shards(): lower_half = side_row(half_system[0, 0], -1).reshape(shard_rows, CHI, HALF)]
    ppermute x4 -> x0, starting transfers between devices: 28.4 us -> none  [passed_along(): return lax.ppermute(x, axis, [(i, (i + by) % size) for i in range(size)])]
  transfers between devices with their start and end apart: 6 -> 0, of which waited for: 4 -> 0; matrix products, arithmetic and copies ran while one was open for 12% -> 0% of each run, Pallas kernels for 0% -> 0%
where the time goes in v1:
time: 150 us; the launch traced here: 149 us
  Pallas kernels  135 us (90%)
  local copies, waits for them, and re-layouts  10 us (7%)
  other arithmetic  3.81 us (3%)
    pallas_call x1, Pallas kernels, absorb_backward(): pl.pallas_call(functools.partial(kernel, nr, nc, ne), out_shape=(jax.Shap...  135 us
    unnamed x10, local copies, waits for them, and re-layouts  7.26 us
    convert_element_type x1, other arithmetic, shards(): jnp.where(out_mask, weight[:, None] * cotangent[0, 0].astype(F32), 0.0)  3.18 us

profile of v1, /device:TPU:1, one launch (start us, length us, event | category | flops | bytes accessed | tf_op | source)
XLA Modules:
  0.0 149.4 jit_solution(7954304714191482889)
XLA Ops:
  0.6 1.2 dynamic-slice_bitcast_fusion.vals
  1.9 0.8 slice_bitcast_fusion.1
  2.6 0.7 broadcast_power_fusion
  3.3 0.1 broadcast_bitcast_fusion.1
  3.4 0.8 broadcast_bitcast_fusion
  4.2 0.6 pad_add_fusion.ch
  4.8 3.2 %fusion.1.gn_in = bf16[1024,1024]{1,0:T(8,128)(2,1)} fusion(bf16[1,1,1024,1024]{3,2,1,0:T(8,128)(2,1)} %param.10, f32[1024]{0:T(1024)S(1)} %bitcast.34, s32[1024]{0:T(1024)S(1)} %get-tuple-element.14, s32[1024]{0:T(1024)S(1)} %get-tuple-element.15), kind=kLoop, calls=%fused_computation.2 | loop fusion | flops 5242880 | bytes 4206592 | tf_op jit(solution)/shard_map/convert_element_type | solution.py:401
  8.0 134.9 %shard_map.93 = (bf16[32,1024]{1,0:T(8,128)(2,1)}, bf16[32,32768]{1,0:T(8,128)(2,1)}, bf16[32,32768]{1,0:T(8,128)(2,1)}, f32[1,32]{1,0:T(1,128)}) custom-call(bf16[1024,1024]{1,0:T(8,128)(2,1)} %bitcast.29, bf16[32,32768]{1,0:T(8,128)(2,1)} %bitcast.30, bf16[32,32768]{1,0:T(8,128)(2,1)} %bitcast.31, bf16[1024,1024]{1,0:T(8,128)(2,1)} %fusion.1.gn_in, ...), custom_call_target="tpu_custom_call" | custom-call | tf_op jit(solution)/shard_map/pallas_call | solution.py:379
  142.9 1.5 copy.17
  144.4 0.0 copy-start
  144.4 3.2 %copy.18 = bf16[1,1,32,32768]{3,2,1,0:T(8,128)(2,1)} copy(bf16[1,1,32,32768]{3,2,1,0:T(8,128)(2,1)} %bitcast.28) | data formatting | bytes 4194304
  147.6 0.0 copy-done
  147.6 0.0 copy-start.1
  147.6 1.3 copy.19
  148.9 0.0 copy-done.1
  148.9 0.5 copy.20
  (1 shorter events, 0.0 us)
Async XLA Ops:
  144.4 3.2 %copy-start = (bf16[32,32768]{1,0:T(8,128)(2,1)S(1)}, bf16[32,32768]{1,0:T(8,128)(2,1)}, u32[]{:S(2)}) copy-start(bf16[32,32768]{1,0:T(8,128)(2,1)} %get-tuple-element.10) | copy-start | bytes 6291460
  147.6 1.3 copy-start.1

commit v2 on v1

--- a/solution.py
+++ b/solution.py
@@ -63,10 +63,10 @@
 
 def kernel(
     nr, nc, ne,
-    corner, te, lh, gn_in, ch, vals,
+    corner, te, lh, cot, vals, par,
     gc_out, ge_out, gh_out, gv_out,
-    TE, GN, LHB, CR, CHR, GFS, R, AS, G, NCP, LHM, GFM, S, LM, F, GCB, P1, P1S, P2, PSA, PSS, PSR,
-    te_sem, in_sem, out_sem, cn_send, cn_recv, ch_send, ch_recv,
+    TE, GN, LHB, CR, CH, CHR, ACC, GFS, R, AS, G, NCP, LHM, GFM, S, LM, F, GCB, P1, P1S, P2, PSA, PSS, PSR,
+    te_sem, ct_sem, in_sem, out_sem, cn_send, cn_recv, ch_send, ch_recv,
     gf_send, gf_recv, ab_send, ab_recv, p1_send, p1_recv, p2_send, p2_recv, ps_send, ps_recv,
 ):
     r, c, e = lax.axis_index("row"), lax.axis_index("col"), lax.axis_index("env")
@@ -88,63 +88,105 @@
         pl.semaphore_signal(barrier, inc=1, device_id=where, device_id_type=MESH)
 
     def greet_env(s):
-        greet(dev(rp, c, s))
         greet(dev(rm, c, s))
 
     def greet_z(s):
         greet(dev(rp, cp, x * NZ + s))
-        greet(dev(rm, cm, x * NZ + s))
 
     def greet_x(s):
         greet(dev(r, c, lax.rem(x + 1 + s, NX) * NZ + z))
 
-    loop(ne, greet_env)
-    loop(NZ, greet_z)
-    loop(NX - 1, greet_x)
-
-    gn_copy = pltpu.make_async_copy(gn_in, GN, in_sem.at[0])
-    gn_copy.start()
+    def turned(m):
+        return lax.rem(e // (ne // QN) + m, QN)
+
+    def load_cot(m):
+        rows = at(turned(m) * QW, QW)
+        pltpu.make_async_copy(cot.at[rows, :], GN.at[rows, :], ct_sem.at[turned(m)]).start()
 
     def load_edge(k):
         pltpu.make_async_copy(
             te.at[:, at(k * CHI, CHI)], TE.at[at(k * ROWS_A, ROWS_A), :], te_sem.at[k // KQ]
         ).start()
 
-    loop(HALF, load_edge)
-    lh_copy = pltpu.make_async_copy(lh, LHB, in_sem.at[1])
+    loop(1, load_cot)
+    loop(KQ, load_edge)
+    loop(ne, greet_env)
+    loop(NZ, greet_z)
+    loop(NX - 1, greet_x)
+    greet(dev(rm, cm, e))
+    loop(QN - 1, lambda m: load_cot(m + 1))
+    loop(HALF - KQ, lambda k: load_edge(k + KQ))
+    lh_copy = pltpu.make_async_copy(lh, LHB, in_sem)
     lh_copy.start()
-    gn_copy.wait()
-
-    pl.semaphore_wait(barrier, 2 * ne + 2 * NZ + NX - 1)
-
-    remote(ch, CHR, ch_send, ch_recv, dev(rp, c, e)).start()
+
+    for role in range(4):
+        for g in range(NBLK):
+            CH[role:role + 1, g * BLK:(g + 1) * BLK] = jnp.broadcast_to(par[role:role + 1, g:g + 1], (1, BLK))
+
+    def weigh(m):
+        rows = at(turned(m) * QW, QW)
+        part = GN.at[rows, :]
+        pltpu.make_async_copy(part, part, ct_sem.at[turned(m)]).wait()
+
+        def block(g):
+            rows = at(turned(m) * QW + g * BLK, BLK)
+            weight = jnp.broadcast_to(lax.rsqrt(vals[0:1, rows]), (BLK, BLK)).T
+            charge = CH[2:3, rows]
+            for t in range(NBLK):
+                lanes = slice(t * BLK, (t + 1) * BLK)
+                keep = charge == CH[3:4, lanes]
+                GN[rows, lanes] = jnp.where(keep, weight * GN[rows, lanes].astype(F32), 0.0).astype(BF16)
+
+        loop(QW // BLK, block)
 
     def send_corner(g):
         rows = at(g * BLK, BLK)
         remote(corner.at[rows, :], CR.at[rows, :], cn_send, cn_recv.at[g], dev(rp, cp, e)).start()
 
-    def edge_chunk(q):
+    def edge_rows(q, m):
+        rows = at(turned(m) * QW, QW)
         cols = at(q * QW, QW)
-        whole = TE.at[cols, :]
-        pltpu.make_async_copy(whole, whole, te_sem.at[q]).wait()
-
-        def rows_of(m):
-            rows = at(m * 256, 256)
-            GFS[rows, cols] = dot_nt(GN[rows, :], TE[cols, :]).astype(BF16)
-
-        loop(CHI // 256, rows_of)
-
+        GFS[rows, cols] = dot_nt(GN[rows, :], TE[cols, :]).astype(BF16)
+
+    def send_full(q, m):
         def send(j):
-            s = lax.rem(e + j, ne)
+            s = turned(m) * (ne // QN) + lax.rem(e + j, ne // QN)
             remote(
-                GFS.at[at(s * ROWS_A, ROWS_A), cols], R.at[at(e * ROWS_A, ROWS_A), cols],
+                GFS.at[at(s * ROWS_A, ROWS_A), at(q * QW, QW)], R.at[at(e * ROWS_A, ROWS_A), at(q * QW, QW)],
                 gf_send.at[q], gf_recv.at[q], dev(rp, c, s),
             ).start()
 
-        loop(ne, send)
-
+        loop(ne // QN, send)
+
+    def edge_ready(q):
+        whole = TE.at[at(q * QW, QW), :]
+        pltpu.make_async_copy(whole, whole, te_sem.at[q]).wait()
+
+    weigh(0)
+    edge_ready(0)
+    edge_rows(0, 0)
+    pl.semaphore_wait(barrier, ne + NZ + NX)
+    send_full(0, 0)
+    remote(CH, CHR, ch_send, ch_recv, dev(rp, c, e)).start()
     loop(NBLK, send_corner)
-    loop(QN, edge_chunk)
+
+    def edge_first(m):
+        weigh(m + 1)
+        edge_rows(0, m + 1)
+        send_full(0, m + 1)
+
+    loop(QN - 1, edge_first)
+
+    def edge_chunk(q):
+        edge_ready(q + 1)
+
+        def part(m):
+            edge_rows(q + 1, m)
+            send_full(q + 1, m)
+
+        loop(QN, part)
+
+    loop(QN - 1, edge_chunk)
 
     lh_copy.wait()
 
@@ -169,6 +211,34 @@
             LHM[rows, t * LANE:(t + 1) * LANE] = LM[t, rows, :].astype(BF16)
 
     loop(HALF, narrow)
+
+    def half_chunk(q):
+        cols = at(q * QW, QW)
+        whole = R.at[:, cols]
+        remote(whole, whole, gf_send.at[q], gf_recv.at[q], dev(rp, c, e)).wait_recv()
+
+        def regroup(d):
+            for k2 in range(KQ // 4):
+                lanes = at(q * QW + k2 * LANE, LANE)
+                mixed = tile_mix([
+                    R[at((d * 4 + d4) * ROWS_A, ROWS_A), lanes].astype(F32) for d4 in range(4)])
+                for k4 in range(4):
+                    GFM[at((q * KQ + k2 * 4 + k4) * ROWS_A, ROWS_A), at(d * LANE, LANE)] = mixed[k4].astype(BF16)
+
+        loop(CHI // LANE, regroup)
+
+        def add(s):
+            rows = at(s * GRP, GRP)
+            ACC[rows, :] = ACC[rows, :] + dot_tn(LHM[cols, rows], GFM[cols, :])
+
+        loop(SUB, add)
+
+    def clear(g):
+        rows = at(g * 32, 32)
+        ACC[rows, :] = jnp.zeros((32, CHI), F32)
+
+    loop(CHI // 32, clear)
+    loop(QN - 1, half_chunk)
 
     remote(CHR, CHR, ch_send, ch_recv, dev(rp, c, e)).wait_recv()
 
@@ -214,50 +284,17 @@
 
     loop(QN, absorb_chunk)
 
-    PSA[...] = jnp.zeros_like(PSA)
-
-    def half_chunk(q):
-        cols = at(q * QW, QW)
-        whole = R.at[:, cols]
-        remote(whole, whole, gf_send.at[q], gf_recv.at[q], dev(rp, c, e)).wait_recv()
-
-        def regroup(d):
-            for k2 in range(KQ // 4):
-                lanes = at(q * QW + k2 * LANE, LANE)
-                tiles = []
-                total = PSA[...]
-                for d4 in range(4):
-                    rows = at((d * 4 + d4) * ROWS_A, ROWS_A)
-                    tile = R[rows, lanes].astype(F32)
-                    total = total + tile * AS[rows, lanes].astype(F32)
-                    tiles.append(tile)
-                PSA[...] = total
-                mixed = tile_mix(tiles)
-                for k4 in range(4):
-                    GFM[at((q * KQ + k2 * 4 + k4) * ROWS_A, ROWS_A), at(d * LANE, LANE)] = mixed[k4].astype(BF16)
-
-        loop(CHI // LANE, regroup)
-
-        def half_cols(n):
-            t = dot_nt(GFM[cols, :], NCP[at(n * 256, 256), :])
-            for h in range(2):
-                LM[n * 2 + h, cols, :] = t[:, h * LANE:(h + 1) * LANE]
-
-        loop(CHI // 256, half_cols)
-
-    loop(QN, half_chunk)
-
-    PSS[...] = jnp.broadcast_to(jnp.sum(PSA[...], axis=1, keepdims=True), (ROWS_A, LANE))
-    ps_copy = remote(PSS, PSR, ps_send, ps_recv, dev(rm, c, e))
-    ps_copy.start()
+    half_chunk(QN - 1)
 
     def corner_part(s):
-        t = dot_tn(LHM[:, at(s * GRP, GRP)], GFM[...])
-        for g in range(NBLK):
+        def block(g):
             for h in range(CHI // LANE):
-                same = CHR[0:1, g * BLK:(g + 1) * BLK] == CHR[1:2, h * LANE:(h + 1) * LANE]
-                part = t[g * (BLK // SUB):(g + 1) * (BLK // SUB), h * LANE:(h + 1) * LANE]
+                lanes = slice(h * LANE, (h + 1) * LANE)
+                same = CHR[0:1, at(g * BLK, BLK)] == CHR[1:2, lanes]
+                part = ACC[at(s * GRP + g * (BLK // SUB), BLK // SUB), lanes]
                 F[h, pl.ds(g * BLK + s, BLK // SUB, stride=SUB), :] = jnp.where(same, part, 0.0)
+
+        loop(NBLK, block)
 
     loop(SUB, corner_part)
 
@@ -276,6 +313,32 @@
         ).start()
 
     loop(NX - 1, send_x)
+
+    def pair(d):
+        rows = at(d * ROWS_A, ROWS_A)
+        total = PSA[...]
+        for t in range(CHI // LANE):
+            lanes = slice(t * LANE, (t + 1) * LANE)
+            total = total + R[rows, lanes].astype(F32) * AS[rows, lanes].astype(F32)
+        PSA[...] = total
+
+    PSA[...] = jnp.zeros_like(PSA)
+    loop(ne, pair)
+    PSS[...] = jnp.broadcast_to(jnp.sum(PSA[...], axis=1, keepdims=True), (ROWS_A, LANE))
+    ps_copy = remote(PSS, PSR, ps_send, ps_recv, dev(rm, c, e))
+    ps_copy.start()
+
+    def half_rows(q):
+        cols = at(q * QW, QW)
+
+        def half_cols(n):
+            t = dot_nt(GFM[cols, :], NCP[at(n * 256, 256), :])
+            for h in range(2):
+                LM[n * 2 + h, cols, :] = t[:, h * LANE:(h + 1) * LANE]
+
+        loop(CHI // 256, half_cols)
+
+    loop(QN, half_rows)
 
     def turn_back(i):
         t = jnp.concatenate([
@@ -291,7 +354,7 @@
             LHB[:, at((g * 8 + u) * LANE, LANE)] = S[at((g * 8 + u) * ROWS_A, ROWS_A), :].astype(BF16)
 
     loop(GRP // 8, gather)
-    gh_copy = pltpu.make_async_copy(LHB, gh_out, in_sem.at[1])
+    gh_copy = pltpu.make_async_copy(LHB, gh_out, in_sem)
     gh_copy.start()
 
     remote(P1, P1, p1_send, p1_recv, dev(r, c, e)).wait_recv()
@@ -341,12 +404,16 @@
         gc_out[:, lanes] = total.astype(BF16)
 
     ps_copy.wait_recv()
-    own = lax.broadcasted_iota(jnp.int32, (ROWS_A, LANE), 0) == lax.broadcasted_iota(jnp.int32, (ROWS_A, LANE), 1)
-    sums = jnp.sum(jnp.where(own, PSR[...], 0.0), axis=0, keepdims=True)
-    gv_out[...] = -0.5 * sums[:, :ROWS_A] / vals[...]
+    row = lax.broadcasted_iota(jnp.int32, (ROWS_A, LANE), 0)
+    lane = lax.broadcasted_iota(jnp.int32, (ROWS_A, LANE), 1)
+    tile = vals[0:1, at((e // (LANE // ROWS_A)) * LANE, LANE)]
+    mine = lane == row + lax.rem(e, LANE // ROWS_A) * ROWS_A
+    value = jnp.sum(jnp.where(mine, jnp.broadcast_to(tile, (ROWS_A, LANE)), 0.0), axis=1, keepdims=True)
+    grads = -0.5 * PSR[...] / value
+    gv_out[...] = jnp.sum(jnp.where(lane == row, grads, 0.0), axis=0, keepdims=True)[:, :ROWS_A]
 
     ps_copy.wait_send()
-    remote(ch, CHR, ch_send, ch_recv, dev(rp, c, e)).wait_send()
+    remote(CH, CHR, ch_send, ch_recv, dev(rp, c, e)).wait_send()
     remote(CR, CR, cn_send, cn_recv.at[0], dev(rp, cp, e)).wait_send()
     for q in range(QN):
         part = GFS.at[:, q * QW:(q + 1) * QW]
@@ -359,21 +426,24 @@
     pltpu.make_async_copy(TE, TE, out_sem).wait()
 
 
-def absorb_backward(sizes, corner, te, lh, gn, ch, vals):
+def absorb_backward(sizes, corner, te, lh, cot, vals, par):
     nr, nc, ne = sizes
-    hbm = pl.BlockSpec(memory_space=pl.ANY)
+    hbm = pl.BlockSpec(memory_space=pltpu.HBM)
+    free = pl.BlockSpec(memory_space=pl.ANY)
     vmem = pl.BlockSpec(memory_space=pltpu.VMEM)
     dma = pltpu.SemaphoreType.DMA
     square = pltpu.VMEM((CHI, CHI), BF16)
     tiles = pltpu.VMEM((CHI // LANE, CHI, LANE), F32)
+    charges = pltpu.VMEM((8, CHI), jnp.int32)
     scratch = [
-        square, square, pltpu.VMEM((ROWS_A, CHI * HALF), BF16), square, pltpu.VMEM((8, CHI), jnp.int32),
+        square, square, pltpu.VMEM((ROWS_A, CHI * HALF), BF16), square, charges, charges,
+        pltpu.VMEM((CHI, CHI), F32),
         square, square, square, square, square, square, square,
         pltpu.VMEM((GRP * ROWS_A, LANE), F32), tiles, tiles, square,
         pltpu.VMEM((NX - 1, CHI // NX, CHI), BF16), pltpu.VMEM((CHI // NX, CHI), BF16),
         pltpu.VMEM((NZ * ROWS_A, CHI), BF16),
         pltpu.VMEM((ROWS_A, LANE), F32), pltpu.VMEM((ROWS_A, LANE), F32), pltpu.VMEM((ROWS_A, LANE), F32),
-        dma((QN,)), dma((2,)), dma, dma, dma((NBLK,)), dma, dma,
+        dma((QN,)), dma((QN,)), dma, dma, dma, dma((NBLK,)), dma, dma,
         dma((QN,)), dma((QN,)), dma((QN,)), dma((QN,)), dma, dma, dma, dma, dma, dma,
     ]
     return pl.pallas_call(
@@ -384,25 +454,18 @@
             jax.ShapeDtypeStruct((ROWS_A, CHI * HALF), BF16),
             jax.ShapeDtypeStruct((1, ROWS_A), F32),
         ),
-        in_specs=[hbm, hbm, hbm, hbm, hbm, vmem],
-        out_specs=(vmem, hbm, hbm, vmem),
+        in_specs=[hbm, hbm, hbm, hbm, vmem, vmem],
+        out_specs=(vmem, free, free, vmem),
         scratch_shapes=scratch,
         compiler_params=pltpu.CompilerParams(
-            collective_id=0, has_side_effects=True, vmem_limit_bytes=60 * 1024 * 1024
+            collective_id=0, has_side_effects=True, vmem_limit_bytes=54 * 1024 * 1024
         ),
-    )(corner, te, lh, gn, ch, vals)
+    )(corner, te, lh, cot, vals, par)
 
 
 def shards(sizes, corner, top_edge, half_system, values, cotangent, parity):
-    rows = top_edge.shape[2]
-    charges = jnp.repeat(parity[0, 0], BLK, axis=1)
-    out_mask = charges[2][:, None] == charges[3][None, :]
-    weight = values[0, 0] ** (-0.5)
-    grad_new = jnp.where(out_mask, weight[:, None] * cotangent[0, 0].astype(F32), 0.0).astype(BF16)
-    ch = jnp.concatenate([charges, charges], axis=0)
-    own = lax.dynamic_slice_in_dim(values[0, 0], lax.axis_index("env") * rows, rows, 0)[None, :]
     gc, ge, gh, gv = absorb_backward(
-        sizes, corner[0, 0], top_edge[0, 0], half_system[0, 0], grad_new, ch, own
+        sizes, corner[0, 0], top_edge[0, 0], half_system[0, 0], cotangent[0, 0], values[0], parity[0, 0]
     )
     return gc[None, None], ge[None, None], gh[None, None], gv[None]
 

time: 150 us -> 136 us (0.907)
  Pallas kernels: 135 us -> 128 us
  other arithmetic: 3.81 us -> 0 us
  local copies, waits for them, and re-layouts: 10 us -> 6.5 us
    pallas_call x1, Pallas kernels: 135 us -> 128 us  [absorb_backward(): pl.pallas_call(functools.partial(kernel, nr, nc, ne), out_shape=(jax.Shap...]
    convert_element_type x1 -> x0, other arithmetic: 3.18 us -> none  [shards(): jnp.where(out_mask, weight[:, None] * cotangent[0, 0].astype(F32), 0.0)]
    unnamed x10 -> x8, local copies, waits for them, and re-layouts: 7.26 us -> 6.5 us
where the time goes in v2:
time: 136 us
  Pallas kernels  128 us (94%)
  local copies, waits for them, and re-layouts  6.5 us (5%)
    pallas_call x1, Pallas kernels, absorb_backward(): pl.pallas_call(functools.partial(kernel, nr, nc, ne), out_shape=(jax.Shap...  128 us
    unnamed x8, local copies, waits for them, and re-layouts  6.5 us

profile of v2, /device:TPU:1, one launch (start us, length us, event | category | flops | bytes accessed | tf_op | source)
XLA Modules:
  0.0 135.6 jit_solution(3364325057880245479)
XLA Ops:
  0.6 128.4 %shard_map.93 = (bf16[32,1024]{1,0:T(8,128)(2,1)}, bf16[32,32768]{1,0:T(8,128)(2,1)}, bf16[32,32768]{1,0:T(8,128)(2,1)}, f32[1,32]{1,0:T(1,128)}) custom-call(bf16[1024,1024]{1,0:T(8,128)(2,1)} %bitcast.12, bf16[32,32768]{1,0:T(8,128)(2,1)} %bitcast.13, bf16[32,32768]{1,0:T(8,128)(2,1)} %bitcast.14, bf16[1024,1024]{1,0:T(8,128)(2,1)} %bitcast.15, ...), custom_call_target="tpu_custom_call" | custom-call | tf_op jit(solution)/shard_map/pallas_call | solution.py:449
  129.1 1.5 %copy.14 = bf16[1,1,32,1024]{3,2,1,0:T(8,128)(2,1)} copy(bf16[1,1,32,1024]{3,2,1,0:T(8,128)(2,1)} %bitcast.16) | data formatting | bytes 131072
  130.5 0.0 copy-start
  130.5 3.2 %copy.15 = bf16[1,1,32,32768]{3,2,1,0:T(8,128)(2,1)} copy(bf16[1,1,32,32768]{3,2,1,0:T(8,128)(2,1)} %bitcast.11) | data formatting | bytes 4194304
  133.7 0.0 copy-done
  133.7 0.0 copy-start.1
  133.7 1.3 copy.16
  135.1 0.0 copy-done.1
  135.1 0.5 copy.17
Async XLA Ops:
  130.5 3.2 %copy-start = (bf16[32,32768]{1,0:T(8,128)(2,1)S(1)}, bf16[32,32768]{1,0:T(8,128)(2,1)}, u32[]{:S(2)}) copy-start(bf16[32,32768]{1,0:T(8,128)(2,1)} %get-tuple-element.10) | copy-start | bytes 6291460
  133.7 1.3 copy-start.1

commit v3 on v2

--- a/solution.py
+++ b/solution.py
@@ -65,8 +65,8 @@
     nr, nc, ne,
     corner, te, lh, cot, vals, par,
     gc_out, ge_out, gh_out, gv_out,
-    TE, GN, LHB, CR, CH, CHR, ACC, GFS, R, AS, G, NCP, LHM, GFM, S, LM, F, GCB, P1, P1S, P2, PSA, PSS, PSR,
-    te_sem, ct_sem, in_sem, out_sem, cn_send, cn_recv, ch_send, ch_recv,
+    TE, GN, LHB, CR, CH, CHR, ACC, GFS, R, G, NCP, LHM, GFM, S, LM, F, P1, P1S, P2, PSA, PSS, PSR,
+    te_sem, ct_sem, in_sem, cn_send, cn_recv, ch_send, ch_recv,
     gf_send, gf_recv, ab_send, ab_recv, p1_send, p1_recv, p2_send, p2_recv, ps_send, ps_recv,
 ):
     r, c, e = lax.axis_index("row"), lax.axis_index("col"), lax.axis_index("env")
@@ -82,6 +82,8 @@
             src_ref=src, dst_ref=dst, send_sem=send, recv_sem=recv, device_id=where, device_id_type=MESH
         )
 
+    AS, GCB = TE, CR
+
     barrier = pltpu.get_barrier_semaphore()
 
     def greet(where):
@@ -108,12 +110,12 @@
             te.at[:, at(k * CHI, CHI)], TE.at[at(k * ROWS_A, ROWS_A), :], te_sem.at[k // KQ]
         ).start()
 
-    loop(1, load_cot)
-    loop(KQ, load_edge)
     loop(ne, greet_env)
     loop(NZ, greet_z)
     loop(NX - 1, greet_x)
     greet(dev(rm, cm, e))
+    loop(1, load_cot)
+    loop(KQ, load_edge)
     loop(QN - 1, lambda m: load_cot(m + 1))
     loop(HALF - KQ, lambda k: load_edge(k + KQ))
     lh_copy = pltpu.make_async_copy(lh, LHB, in_sem)
@@ -139,9 +141,24 @@
 
         loop(QW // BLK, block)
 
-    def send_corner(g):
-        rows = at(g * BLK, BLK)
-        remote(corner.at[rows, :], CR.at[rows, :], cn_send, cn_recv.at[g], dev(rp, cp, e)).start()
+    odd = lax.rem(x, 2)
+    first = [2 * odd, 6 - 2 * odd, 2 * odd + 1, 7 - 2 * odd]
+    right, left = lax.rem(x + 1, NX), lax.rem(x + NX - 1, NX)
+    near = jnp.where(odd == 0, right, left)
+    far = jnp.where(odd == 0, left, right)
+
+    def send_corner():
+        for g in first:
+            rows = at(g * BLK, BLK)
+            remote(corner.at[rows, :], CR.at[rows, :], cn_send, cn_recv.at[g], dev(rp, cp, e)).start()
+
+    def forward_corner():
+        for n, g in enumerate(first):
+            part = CR.at[at(g * BLK, BLK), :]
+            to = dev(r, c, (near if n % 2 == 0 else far) * NZ + z)
+            copy = remote(part, part, cn_send, cn_recv.at[g], to)
+            copy.wait_recv()
+            copy.start()
 
     def edge_rows(q, m):
         rows = at(turned(m) * QW, QW)
@@ -168,7 +185,7 @@
     pl.semaphore_wait(barrier, ne + NZ + NX)
     send_full(0, 0)
     remote(CH, CHR, ch_send, ch_recv, dev(rp, c, e)).start()
-    loop(NBLK, send_corner)
+    send_corner()
 
     def edge_first(m):
         weigh(m + 1)
@@ -211,6 +228,7 @@
             LHM[rows, t * LANE:(t + 1) * LANE] = LM[t, rows, :].astype(BF16)
 
     loop(HALF, narrow)
+    forward_corner()
 
     def half_chunk(q):
         cols = at(q * QW, QW)
@@ -244,8 +262,12 @@
 
     def corner_rows(g):
         rows = at(g * BLK, BLK)
-        part = CR.at[rows, :]
-        remote(part, part, cn_send, cn_recv.at[g], dev(rp, cp, e)).wait_recv()
+
+        @pl.when(jnp.logical_and(g // 2 != odd, g // 2 != 3 - odd))
+        def _():
+            part = CR.at[rows, :]
+            remote(part, part, cn_send, cn_recv.at[g], dev(rp, cp, e)).wait_recv()
+
         charge = CHR[0:1, rows]
         for t in range(CHI // LANE):
             lanes = slice(t * LANE, (t + 1) * LANE)
@@ -273,6 +295,9 @@
 
         loop(CHI // 256, columns_of)
 
+    def absorb_send(q):
+        cols = at(q * QW, QW)
+
         def send(j):
             s = lax.rem(e + j, ne)
             remote(
@@ -282,7 +307,8 @@
 
         loop(ne, send)
 
-    loop(QN, absorb_chunk)
+    absorb_chunk(0)
+    absorb_send(0)
 
     half_chunk(QN - 1)
 
@@ -298,6 +324,8 @@
 
     loop(SUB, corner_part)
 
+    remote(CR, CR, cn_send, cn_recv.at[0], dev(rp, cp, e)).wait_send()
+
     def corner_narrow(g):
         rows = at(g * 32, 32)
         for t in range(CHI // LANE):
@@ -313,6 +341,12 @@
         ).start()
 
     loop(NX - 1, send_x)
+
+    def absorb_more(q):
+        absorb_chunk(q + 1)
+        absorb_send(q + 1)
+
+    loop(QN - 1, absorb_more)
 
     def pair(d):
         rows = at(d * ROWS_A, ROWS_A)
@@ -351,11 +385,9 @@
 
     def gather(g):
         for u in range(8):
-            LHB[:, at((g * 8 + u) * LANE, LANE)] = S[at((g * 8 + u) * ROWS_A, ROWS_A), :].astype(BF16)
+            gh_out[:, at((g * 8 + u) * LANE, LANE)] = S[at((g * 8 + u) * ROWS_A, ROWS_A), :].astype(BF16)
 
     loop(GRP // 8, gather)
-    gh_copy = pltpu.make_async_copy(LHB, gh_out, in_sem)
-    gh_copy.start()
 
     remote(P1, P1, p1_send, p1_recv, dev(r, c, e)).wait_recv()
 
@@ -383,15 +415,7 @@
         cols = at(q * QW, QW)
         whole = G.at[:, cols]
         remote(whole, whole, ab_send.at[q], ab_recv.at[q], dev(rm, c, e)).wait_recv()
-        TE[cols, :] = dot_tn(G[:, cols], GN[...]).astype(BF16)
-
-        def store(j):
-            k = q * KQ + j
-            pltpu.make_async_copy(
-                TE.at[at(k * ROWS_A, ROWS_A), :], ge_out.at[:, at(k * CHI, CHI)], out_sem
-            ).start()
-
-        loop(KQ, store)
+        ge_out[cols, :] = dot_tn(G[:, cols], GN[...]).astype(BF16)
 
     loop(QN, edge_grad)
 
@@ -414,7 +438,6 @@
 
     ps_copy.wait_send()
     remote(CH, CHR, ch_send, ch_recv, dev(rp, c, e)).wait_send()
-    remote(CR, CR, cn_send, cn_recv.at[0], dev(rp, cp, e)).wait_send()
     for q in range(QN):
         part = GFS.at[:, q * QW:(q + 1) * QW]
         remote(part, part, gf_send.at[q], gf_recv.at[q], dev(rp, c, e)).wait_send()
@@ -422,14 +445,11 @@
         remote(part, part, ab_send.at[q], ab_recv.at[q], dev(rm, c, e)).wait_send()
     remote(P1, P1, p1_send, p1_recv, dev(r, c, e)).wait_send()
     remote(P1S, P1S, p2_send, p2_recv, dev(rm, cm, e)).wait_send()
-    gh_copy.wait()
-    pltpu.make_async_copy(TE, TE, out_sem).wait()
 
 
 def absorb_backward(sizes, corner, te, lh, cot, vals, par):
     nr, nc, ne = sizes
     hbm = pl.BlockSpec(memory_space=pltpu.HBM)
-    free = pl.BlockSpec(memory_space=pl.ANY)
     vmem = pl.BlockSpec(memory_space=pltpu.VMEM)
     dma = pltpu.SemaphoreType.DMA
     square = pltpu.VMEM((CHI, CHI), BF16)
@@ -438,35 +458,69 @@
     scratch = [
         square, square, pltpu.VMEM((ROWS_A, CHI * HALF), BF16), square, charges, charges,
         pltpu.VMEM((CHI, CHI), F32),
-        square, square, square, square, square, square, square,
-        pltpu.VMEM((GRP * ROWS_A, LANE), F32), tiles, tiles, square,
+        square, square, square, square, square, square,
+        pltpu.VMEM((GRP * ROWS_A, LANE), F32), tiles, tiles,
         pltpu.VMEM((NX - 1, CHI // NX, CHI), BF16), pltpu.VMEM((CHI // NX, CHI), BF16),
         pltpu.VMEM((NZ * ROWS_A, CHI), BF16),
         pltpu.VMEM((ROWS_A, LANE), F32), pltpu.VMEM((ROWS_A, LANE), F32), pltpu.VMEM((ROWS_A, LANE), F32),
-        dma((QN,)), dma((QN,)), dma, dma, dma, dma((NBLK,)), dma, dma,
+        dma((QN,)), dma((QN,)), dma, dma, dma((NBLK,)), dma, dma,
         dma((QN,)), dma((QN,)), dma((QN,)), dma((QN,)), dma, dma, dma, dma, dma, dma,
     ]
     return pl.pallas_call(
         functools.partial(kernel, nr, nc, ne),
+        out_shape=(
+            pltpu.VMEM((ROWS_A, CHI), BF16),
+            pltpu.VMEM((CHI, CHI), BF16),
+            pltpu.VMEM((ROWS_A, CHI * HALF), BF16),
+            pltpu.VMEM((1, ROWS_A), F32),
+        ),
+        in_specs=[hbm, hbm, hbm, hbm, vmem, vmem],
+        out_specs=(vmem, vmem, vmem, vmem),
+        scratch_shapes=scratch,
+        compiler_params=pltpu.CompilerParams(
+            collective_id=0, has_side_effects=True, vmem_limit_bytes=58 * 1024 * 1024
+        ),
+    )(corner, te, lh, cot, vals, par)
+
+
+def store_kernel(gc, ge, gh, gv, gc_out, ge_out, gh_out, gv_out, sem):
+    def edge(k):
+        return pltpu.make_async_copy(
+            ge.at[at(k * ROWS_A, ROWS_A), :], ge_out.at[:, at(k * CHI, CHI)], sem.at[0])
+
+    loop(HALF, lambda k: edge(k).start())
+    rest = [
+        pltpu.make_async_copy(src, dst, sem.at[1 + n])
+        for n, (src, dst) in enumerate(((gh, gh_out), (gc, gc_out), (gv, gv_out)))]
+    for copy in rest:
+        copy.start()
+    pltpu.make_async_copy(ge, ge, sem.at[0]).wait()
+    for copy in rest:
+        copy.wait()
+
+
+def store(gc, ge, gh, gv):
+    vmem = pl.BlockSpec(memory_space=pltpu.VMEM)
+    hbm = pl.BlockSpec(memory_space=pltpu.HBM)
+    return pl.pallas_call(
+        store_kernel,
         out_shape=(
             jax.ShapeDtypeStruct((ROWS_A, CHI), BF16),
             jax.ShapeDtypeStruct((ROWS_A, HALF * CHI), BF16),
             jax.ShapeDtypeStruct((ROWS_A, CHI * HALF), BF16),
             jax.ShapeDtypeStruct((1, ROWS_A), F32),
         ),
-        in_specs=[hbm, hbm, hbm, hbm, vmem, vmem],
-        out_specs=(vmem, free, free, vmem),
-        scratch_shapes=scratch,
-        compiler_params=pltpu.CompilerParams(
-            collective_id=0, has_side_effects=True, vmem_limit_bytes=54 * 1024 * 1024
-        ),
-    )(corner, te, lh, cot, vals, par)
+        in_specs=[vmem] * 4,
+        out_specs=(hbm,) * 4,
+        scratch_shapes=[pltpu.SemaphoreType.DMA((4,))],
+        compiler_params=pltpu.CompilerParams(vmem_limit_bytes=16 * 1024 * 1024),
+    )(*(pltpu.with_memory_space_constraint(t, pltpu.VMEM) for t in (gc, ge, gh, gv)))
 
 
 def shards(sizes, corner, top_edge, half_system, values, cotangent, parity):
-    gc, ge, gh, gv = absorb_backward(
+    gc, ge, gh, gv = store(*absorb_backward(
         sizes, corner[0, 0], top_edge[0, 0], half_system[0, 0], cotangent[0, 0], values[0], parity[0, 0]
-    )
+    ))
     return gc[None, None], ge[None, None], gh[None, None], gv[None]
 
 

time: 136 us -> 125 us (0.919)
  local copies, waits for them, and re-layouts: 6.5 us -> 0 us
  Pallas kernels: 128 us -> 124 us
    unnamed x8 -> x0, local copies, waits for them, and re-layouts: 6.5 us -> none
    pallas_call x1 -> x2, Pallas kernels: 128 us -> 124 us  [the longest x1 122 us: absorb_backward(): pl.pallas_call(functools.partial(kernel, nr, nc, ne), out_shape=(pltpu.VM...]
where the time goes in v3:
time: 125 us
  Pallas kernels  124 us (99%)
    pallas_call x1, Pallas kernels, absorb_backward(): pl.pallas_call(functools.partial(kernel, nr, nc, ne), out_shape=(pltpu.VM...  122 us

profile of v3, /device:TPU:1, one launch (start us, length us, event | category | flops | bytes accessed | tf_op | source)
XLA Modules:
  0.0 124.9 jit_solution(2058316725992029162)
XLA Ops:
  0.6 122.2 %shard_map.93 = (bf16[32,1024]{1,0:T(8,128)(2,1)S(1)}, bf16[1024,1024]{1,0:T(8,128)(2,1)S(1)}, bf16[32,32768]{1,0:T(8,128)(2,1)S(1)}, f32[1,32]{1,0:T(1,128)S(1)}) custom-call(bf16[1024,1024]{1,0:T(8,128)(2,1)} %bitcast.10, bf16[32,32768]{1,0:T(8,128)(2,1)} %bitcast.11, bf16[32,32768]{1,0:T(8,128)(2,1)} %bitcast.12, bf16[1024,1024]{1,0:T(8,128)(2,1)} %bitcast.13, ...), custom_call_target="tpu_custom_call" | custom-call | tf_op jit(solution)/shard_map/pallas_call | solution.py:469
  122.9 2.0 %shard_map.94 = (bf16[32,1024]{1,0:T(8,128)(2,1)}, bf16[32,32768]{1,0:T(8,128)(2,1)}, bf16[32,32768]{1,0:T(8,128)(2,1)}, f32[1,32]{1,0:T(1,128)}) custom-call(bf16[32,1024]{1,0:T(8,128)(2,1)S(1)} %get-tuple-element.12.gc, bf16[1024,1024]{1,0:T(8,128)(2,1)S(1)} %get-tuple-element.13.ge, bf16[32,32768]{1,0:T(8,128)(2,1)S(1)} %get-tuple-element.14.gh, ...), custom_call_target="tpu_custom_call" | custom-call | tf_op jit(solution)/shard_map/pallas_call | solution.py:505

commit v4 on v3

--- a/solution.py
+++ b/solution.py
@@ -65,9 +65,9 @@
     nr, nc, ne,
     corner, te, lh, cot, vals, par,
     gc_out, ge_out, gh_out, gv_out,
-    TE, GN, LHB, CR, CH, CHR, ACC, GFS, R, G, NCP, LHM, GFM, S, LM, F, P1, P1S, P2, PSA, PSS, PSR,
+    TE, GN, LHB, CR, CH, CHR, ACC, GFS, R, G, NCP, LHM, GFM, S, LM, F, P1, P1S, PT, PU, P2, PSA, PSS, PSR,
     te_sem, ct_sem, in_sem, cn_send, cn_recv, ch_send, ch_recv,
-    gf_send, gf_recv, ab_send, ab_recv, p1_send, p1_recv, p2_send, p2_recv, ps_send, ps_recv,
+    gf_send, gf_recv, ab_send, ab_recv, p1_send, p1_recv, pt_send, pt_recv, p2_send, p2_recv, ps_send, ps_recv,
 ):
     r, c, e = lax.axis_index("row"), lax.axis_index("col"), lax.axis_index("env")
     rp, rm = lax.rem(r + 1, nr), lax.rem(r + nr - 1, nr)
@@ -114,6 +114,8 @@
     loop(NZ, greet_z)
     loop(NX - 1, greet_x)
     greet(dev(rm, cm, e))
+    greet(dev(r, c, x * NZ + lax.rem(z + 1, NZ)))
+    greet(dev(r, c, x * NZ + lax.rem(z + NZ - 1, NZ)))
     loop(1, load_cot)
     loop(KQ, load_edge)
     loop(QN - 1, lambda m: load_cot(m + 1))
@@ -182,7 +184,7 @@
     weigh(0)
     edge_ready(0)
     edge_rows(0, 0)
-    pl.semaphore_wait(barrier, ne + NZ + NX)
+    pl.semaphore_wait(barrier, ne + NZ + NX + 2)
     send_full(0, 0)
     remote(CH, CHR, ch_send, ch_recv, dev(rp, c, e)).start()
     send_corner()
@@ -295,20 +297,22 @@
 
         loop(CHI // 256, columns_of)
 
-    def absorb_send(q):
+    def absorb_to(q, s):
         cols = at(q * QW, QW)
-
-        def send(j):
-            s = lax.rem(e + j, ne)
-            remote(
-                AS.at[at(s * ROWS_A, ROWS_A), cols], G.at[at(e * ROWS_A, ROWS_A), cols],
-                ab_send.at[q], ab_recv.at[q], dev(rm, c, s),
-            ).start()
-
-        loop(ne, send)
+        remote(
+            AS.at[at(s * ROWS_A, ROWS_A), cols], G.at[at(e * ROWS_A, ROWS_A), cols],
+            ab_send.at[q], ab_recv.at[q], dev(rm, c, s),
+        ).start()
+
+    def absorb_same_x(q):
+        loop(NZ, lambda j: absorb_to(q, x * NZ + lax.rem(z + j, NZ)))
+
+    def absorb_other_x(q):
+        loop(ne - NZ, lambda j: absorb_to(q, lax.rem(x + 1 + j // NZ, NX) * NZ + lax.rem(z + j, NZ)))
 
     absorb_chunk(0)
-    absorb_send(0)
+    absorb_other_x(0)
+    absorb_same_x(0)
 
     half_chunk(QN - 1)
 
@@ -344,9 +348,10 @@
 
     def absorb_more(q):
         absorb_chunk(q + 1)
-        absorb_send(q + 1)
+        absorb_same_x(q + 1)
 
     loop(QN - 1, absorb_more)
+    loop(QN - 1, lambda q: absorb_other_x(q + 1))
 
     def pair(d):
         rows = at(d * ROWS_A, ROWS_A)
@@ -395,21 +400,28 @@
         rows = at(g * 32, 32)
         for t in range(CHI // LANE):
             lanes = slice(t * LANE, (t + 1) * LANE)
-            total = F[t, at(x * span + g * 32, 32), :]
+            mine = at(x * span + g * 32, 32)
+            total = F[t, mine, :]
             for j in range(NX - 1):
                 total = total + P1[j, rows, lanes].astype(F32)
+            F[t, mine, :] = total
             P1S[rows, lanes] = total.astype(BF16)
 
     loop(span // 32, sum_x)
 
-    def send_z(j):
-        to = lax.rem(z + j, NZ)
+    wide = CHI // 2
+    parts = [(h, t) for h in range(2) for t in range(NZ // 2)]
+    sign = [2 * lax.rem(z, 2) - 1, 1 - 2 * lax.rem(z, 2)]
+
+    def owner(h, t):
+        return lax.rem(z + sign[h] * t + NZ, NZ)
+
+    for h, t in parts:
         remote(
-            P1S.at[at(to * ROWS_A, ROWS_A), :], P2.at[at(z * ROWS_A, ROWS_A), :],
-            p2_send, p2_recv, dev(rm, cm, x * NZ + to),
+            P1S.at[at(owner(h, -1 - t) * ROWS_A, ROWS_A), h * wide:(h + 1) * wide],
+            PT.at[(h * 4 + t) * ROWS_A:(h * 4 + t + 1) * ROWS_A, :],
+            pt_send, pt_recv, dev(r, c, x * NZ + owner(h, -1)),
         ).start()
-
-    loop(NZ, send_z)
 
     def edge_grad(q):
         cols = at(q * QW, QW)
@@ -417,13 +429,26 @@
         remote(whole, whole, ab_send.at[q], ab_recv.at[q], dev(rm, c, e)).wait_recv()
         ge_out[cols, :] = dot_tn(G[:, cols], GN[...]).astype(BF16)
 
-    loop(QN, edge_grad)
+    edge_grad(0)
+    remote(PT, PT, pt_send, pt_recv, dev(r, c, e)).wait_recv()
+    for h, t in parts:
+        rows = slice((h * 4 + t) * ROWS_A, (h * 4 + t + 1) * ROWS_A)
+        mine = at(x * span + owner(h, t) * ROWS_A, ROWS_A)
+        for n in range(wide // LANE):
+            lanes = slice(n * LANE, (n + 1) * LANE)
+            PU[rows, lanes] = (F[h * (wide // LANE) + n, mine, :] + PT[rows, lanes].astype(F32)).astype(BF16)
+        remote(
+            PU.at[rows, :], P2.at[t * ROWS_A:(t + 1) * ROWS_A, h * wide:(h + 1) * wide],
+            p2_send, p2_recv, dev(rm, cm, x * NZ + owner(h, t)),
+        ).start()
+
+    loop(QN - 1, lambda q: edge_grad(q + 1))
 
     remote(P2, P2, p2_send, p2_recv, dev(rm, cm, e)).wait_recv()
     for t in range(CHI // LANE):
         lanes = slice(t * LANE, (t + 1) * LANE)
         total = P2[0:ROWS_A, lanes].astype(F32)
-        for j in range(1, NZ):
+        for j in range(1, NZ // 2):
             total = total + P2[j * ROWS_A:(j + 1) * ROWS_A, lanes].astype(F32)
         gc_out[:, lanes] = total.astype(BF16)
 
@@ -444,7 +469,8 @@
         part = AS.at[:, q * QW:(q + 1) * QW]
         remote(part, part, ab_send.at[q], ab_recv.at[q], dev(rm, c, e)).wait_send()
     remote(P1, P1, p1_send, p1_recv, dev(r, c, e)).wait_send()
-    remote(P1S, P1S, p2_send, p2_recv, dev(rm, cm, e)).wait_send()
+    remote(PT, PT, pt_send, pt_recv, dev(r, c, e)).wait_send()
+    remote(PU, PU, p2_send, p2_recv, dev(rm, cm, e)).wait_send()
 
 
 def absorb_backward(sizes, corner, te, lh, cot, vals, par):
@@ -461,10 +487,11 @@
         square, square, square, square, square, square,
         pltpu.VMEM((GRP * ROWS_A, LANE), F32), tiles, tiles,
         pltpu.VMEM((NX - 1, CHI // NX, CHI), BF16), pltpu.VMEM((CHI // NX, CHI), BF16),
-        pltpu.VMEM((NZ * ROWS_A, CHI), BF16),
+        pltpu.VMEM((NZ * ROWS_A, CHI // 2), BF16), pltpu.VMEM((NZ * ROWS_A, CHI // 2), BF16),
+        pltpu.VMEM((NZ // 2 * ROWS_A, CHI), BF16),
         pltpu.VMEM((ROWS_A, LANE), F32), pltpu.VMEM((ROWS_A, LANE), F32), pltpu.VMEM((ROWS_A, LANE), F32),
         dma((QN,)), dma((QN,)), dma, dma, dma((NBLK,)), dma, dma,
-        dma((QN,)), dma((QN,)), dma((QN,)), dma((QN,)), dma, dma, dma, dma, dma, dma,
+        dma((QN,)), dma((QN,)), dma((QN,)), dma((QN,)), dma, dma, dma, dma, dma, dma, dma, dma,
     ]
     return pl.pallas_call(
         functools.partial(kernel, nr, nc, ne),

time: 125 us -> 122 us (0.976)
  Pallas kernels: 124 us -> 122 us
    pallas_call x1, Pallas kernels: 122 us -> 120 us  [absorb_backward(): pl.pallas_call(functools.partial(kernel, nr, nc, ne), out_shape=(pltpu.VM...]
where the time goes in v4:
time: 122 us
  Pallas kernels  122 us (100%)
    pallas_call x1, Pallas kernels, absorb_backward(): pl.pallas_call(functools.partial(kernel, nr, nc, ne), out_shape=(pltpu.VM...  120 us

profile of v4, /device:TPU:1, one launch (start us, length us, event | category | flops | bytes accessed | tf_op | source)
XLA Modules:
  0.0 122.2 jit_solution(5718783270981570794)
XLA Ops:
  0.6 119.5 %shard_map.93 = (bf16[32,1024]{1,0:T(8,128)(2,1)S(1)}, bf16[1024,1024]{1,0:T(8,128)(2,1)S(1)}, bf16[32,32768]{1,0:T(8,128)(2,1)S(1)}, f32[1,32]{1,0:T(1,128)S(1)}) custom-call(bf16[1024,1024]{1,0:T(8,128)(2,1)} %bitcast.10, bf16[32,32768]{1,0:T(8,128)(2,1)} %bitcast.11, bf16[32,32768]{1,0:T(8,128)(2,1)} %bitcast.12, bf16[1024,1024]{1,0:T(8,128)(2,1)} %bitcast.13, ...), custom_call_target="tpu_custom_call" | custom-call | tf_op jit(solution)/shard_map/pallas_call | solution.py:496
  120.1 2.0 %shard_map.94 = (bf16[32,1024]{1,0:T(8,128)(2,1)}, bf16[32,32768]{1,0:T(8,128)(2,1)}, bf16[32,32768]{1,0:T(8,128)(2,1)}, f32[1,32]{1,0:T(1,128)}) custom-call(bf16[32,1024]{1,0:T(8,128)(2,1)S(1)} %get-tuple-element.12.gc, bf16[1024,1024]{1,0:T(8,128)(2,1)S(1)} %get-tuple-element.13.ge, bf16[32,32768]{1,0:T(8,128)(2,1)S(1)} %get-tuple-element.14.gh, ...), custom_call_target="tpu_custom_call" | custom-call | tf_op jit(solution)/shard_map/pallas_call | solution.py:532

commit v5 on v4

--- a/solution.py
+++ b/solution.py
@@ -118,10 +118,6 @@
     greet(dev(r, c, x * NZ + lax.rem(z + NZ - 1, NZ)))
     loop(1, load_cot)
     loop(KQ, load_edge)
-    loop(QN - 1, lambda m: load_cot(m + 1))
-    loop(HALF - KQ, lambda k: load_edge(k + KQ))
-    lh_copy = pltpu.make_async_copy(lh, LHB, in_sem)
-    lh_copy.start()
 
     for role in range(4):
         for g in range(NBLK):
@@ -186,6 +182,10 @@
     edge_rows(0, 0)
     pl.semaphore_wait(barrier, ne + NZ + NX + 2)
     send_full(0, 0)
+    loop(QN - 1, lambda m: load_cot(m + 1))
+    loop(HALF - KQ, lambda k: load_edge(k + KQ))
+    lh_copy = pltpu.make_async_copy(lh, LHB, in_sem)
+    lh_copy.start()
     remote(CH, CHR, ch_send, ch_recv, dev(rp, c, e)).start()
     send_corner()
 

time: 122 us -> 122 us (level)
  no operation moved by 1% of the time
where the time goes in v5:
time: 122 us
  Pallas kernels  121 us (99%)
    pallas_call x1, Pallas kernels, absorb_backward(): pl.pallas_call(functools.partial(kernel, nr, nc, ne), out_shape=(pltpu.VM...  119 us

profile of v5, /device:TPU:1, one launch (start us, length us, event | category | flops | bytes accessed | tf_op | source)
XLA Modules:
  0.0 122.1 jit_solution(1634120231344428271)
XLA Ops:
  0.6 119.4 %shard_map.93 = (bf16[32,1024]{1,0:T(8,128)(2,1)S(1)}, bf16[1024,1024]{1,0:T(8,128)(2,1)S(1)}, bf16[32,32768]{1,0:T(8,128)(2,1)S(1)}, f32[1,32]{1,0:T(1,128)S(1)}) custom-call(bf16[1024,1024]{1,0:T(8,128)(2,1)} %bitcast.10, bf16[32,32768]{1,0:T(8,128)(2,1)} %bitcast.11, bf16[32,32768]{1,0:T(8,128)(2,1)} %bitcast.12, bf16[1024,1024]{1,0:T(8,128)(2,1)} %bitcast.13, ...), custom_call_target="tpu_custom_call" | custom-call | tf_op jit(solution)/shard_map/pallas_call | solution.py:496
  120.0 2.0 %shard_map.94 = (bf16[32,1024]{1,0:T(8,128)(2,1)}, bf16[32,32768]{1,0:T(8,128)(2,1)}, bf16[32,32768]{1,0:T(8,128)(2,1)}, f32[1,32]{1,0:T(1,128)}) custom-call(bf16[32,1024]{1,0:T(8,128)(2,1)S(1)} %get-tuple-element.12.gc, bf16[1024,1024]{1,0:T(8,128)(2,1)S(1)} %get-tuple-element.13.ge, bf16[32,32768]{1,0:T(8,128)(2,1)S(1)} %get-tuple-element.14.gh, ...), custom_call_target="tpu_custom_call" | custom-call | tf_op jit(solution)/shard_map/pallas_call | solution.py:532
